TPU v7x, 128 devices: a whole 4x4x4 slice. The times are simulated.
128 devices in a mesh: seq: 32 (over y_lo, x, z), head: 4 (over y_hi, core).
Axes of the slice: x: 4, y: 4 (y_hi: 2, y_lo: 2; y = y_hi * 2 + y_lo), z: 4, core: 2. Of those that a mesh axis runs over, the one named last changes fastest.
Arguments:
- queries: bfloat16 [16384, 4096], P(('seq', 'head')), may hold values from -8 to 8
- keys: bfloat16 [16384, 2048], P(('seq', 'head')), may hold values from -8 to 8
- values: bfloat16 [16384, 2048], P(('seq', 'head')), may hold values from -6 to 6
- output_cotangent: bfloat16 [16384, 4096], P(('seq', 'head')), may hold values from -6 to 6
Outputs:
- attended: bfloat16 [16384, 4096], P(('seq', 'head'))
- grad_queries: bfloat16 [16384, 4096], P(('seq', 'head'))
- key_gradient: bfloat16 [16384, 2048], P(('seq', 'head'))
- value_gradient: bfloat16 [16384, 2048], P(('seq', 'head'))
All inputs are finite; a program needn't handle non-finite values.
Results may differ from a plain program's by a relative error of at most 0.0095.
Values may be sent and summed in bfloat16 or wider, within the bound.
No kernel may reach another device: no remote copies, remote signals or barrier semaphores. Data moves between devices by JAX's collectives and lax.ppermute only.
A program may use at most 128 MiB of HBM per device.

v0:
```python
import jax
import jax.numpy as jnp
from jax import lax
from jax.experimental import pallas as pl
from jax.experimental.pallas import tpu as pltpu
from jax.sharding import Mesh, PartitionSpec as P


D = 128
WINDOW = 1024
BLOCK = 256
CHUNKS = WINDOW // BLOCK
SPAN = WINDOW + BLOCK
SCALE = 168.0 ** (-0.5)
RATE = SCALE * 1.4426950408889634
BF = jnp.bfloat16
F32 = jnp.float32


def cost(flops, bytes_accessed, transcendentals=0):
    return pl.CostEstimate(flops=int(flops), bytes_accessed=int(bytes_accessed), transcendentals=int(transcendentals))


VMEM = pl.BlockSpec(memory_space=pltpu.VMEM)
SMEM = pl.BlockSpec(memory_space=pltpu.SMEM)
AWAY = pl.BlockSpec(memory_space=pl.ANY)
SUMS = (2, D, 2 * WINDOW)


PIECES = 4


def strips(cuts, heads):
    for j in range(heads):
        at = 0
        for i, per, start, w in cuts:
            yield j, i, j * per + start, at, w
            at += w


def pack(arrays, cuts, heads):
    rows, total, n = arrays[0].shape[0], sum(cut[3] for cut in cuts), len(arrays)

    def kernel(*refs):
        src, out, held, made, sems = refs[:n], refs[n], refs[n + 1 : -2], refs[-2], refs[-1]
        copies = []
        for p in range(PIECES):
            for i in range(n):
                w = arrays[i].shape[1] // PIECES
                copies.append(pltpu.make_async_copy(src[i].at[:, pl.ds(p * w, w)], held[i].at[:, pl.ds(p * w, w)], sems.at[p * n + i]))
        for copy in copies:
            copy.start()
        outs = []
        some = heads // PIECES
        for p in range(PIECES):
            for copy in copies[p * n : (p + 1) * n]:
                copy.wait()
            for j, i, there, here, w in strips(cuts, heads):
                if j // some == p:
                    made[j, :, here : here + w] = held[i][:, there : there + w]
            outs.append(pltpu.make_async_copy(made.at[pl.ds(p * some, some)], out.at[pl.ds(p * some, some)], sems.at[PIECES * n + p]))
            outs[-1].start()
        for copy in outs:
            copy.wait()

    return pl.pallas_call(
        kernel,
        in_specs=[AWAY] * n,
        out_specs=AWAY,
        out_shape=pltpu.HBM((heads, rows, total), arrays[0].dtype),
        scratch_shapes=[pltpu.VMEM(x.shape, x.dtype) for x in arrays]
        + [pltpu.VMEM((heads, rows, total), arrays[0].dtype), pltpu.SemaphoreType.DMA((PIECES * (n + 1),))],
        compiler_params=pltpu.CompilerParams(vmem_limit_bytes=20 * 1024 * 1024),
        cost_estimate=cost(0, 4 * heads * rows * total),
        name="pack",
    )(*[pltpu.with_memory_space_constraint(x, pltpu.HBM) for x in arrays])


def unpack(chunks, cuts, columns):
    heads, rows, _ = chunks[0].shape
    m, n = len(chunks), len(columns)
    shapes = [jax.ShapeDtypeStruct((rows, heads * w), chunks[0].dtype) for w in columns]

    def kernel(*refs):
        src, out, held, sems = refs[:m], refs[m : m + n], refs[m + n : -1], refs[-1]
        copies = []
        for p in range(PIECES):
            for c in range(m):
                for j, i, there, here, w in strips(cuts[c], heads):
                    if j * PIECES // heads == p:
                        held[i][:, there : there + w] = src[c][j, :, here : here + w]
            for i in range(n):
                w = shapes[i].shape[1] // PIECES
                copies.append(pltpu.make_async_copy(held[i].at[:, pl.ds(p * w, w)], out[i].at[:, pl.ds(p * w, w)], sems.at[p * n + i]))
                copies[-1].start()
        for copy in copies:
            copy.wait()

    return pl.pallas_call(
        kernel,
        in_specs=[VMEM] * m,
        out_specs=[AWAY] * n,
        out_shape=shapes,
        scratch_shapes=[pltpu.VMEM(x.shape, x.dtype) for x in shapes]
        + [pltpu.SemaphoreType.DMA((PIECES * n,))],
        compiler_params=pltpu.CompilerParams(vmem_limit_bytes=16 * 1024 * 1024),
        cost_estimate=cost(0, 4 * sum(x.size for x in chunks)),
        name="unpack",
    )(*chunks)


def stage(x):
    def kernel(src, out, sem):
        copy = pltpu.make_async_copy(src, out, sem.at[0])
        copy.start()
        copy.wait()

    return pl.pallas_call(
        kernel,
        in_specs=[AWAY],
        out_specs=VMEM,
        out_shape=jax.ShapeDtypeStruct(x.shape, x.dtype),
        scratch_shapes=[pltpu.SemaphoreType.DMA((1,))],
        compiler_params=pltpu.CompilerParams(vmem_limit_bytes=20 * 1024 * 1024),
        cost_estimate=cost(0, 4 * x.size),
        name="stage",
    )(pltpu.with_memory_space_constraint(x, pltpu.HBM))


def dot(a, b, ca, cb):
    return lax.dot_general(a, b, (((ca,), (cb,)), ((), ())), preferred_element_type=F32)


def fold(x, op):
    y = x[:, 0:D]
    for i in range(1, BLOCK // D):
        y = op(y, x[:, i * D : (i + 1) * D])
    return y


def attend(q, read_g, keys, values, old, hide):
    s = dot(q, keys, 1, 1)
    first = jnp.where(old, s[:, 0:BLOCK] if hide is None else s[:, 0:BLOCK] - hide[0], s[:, WINDOW:SPAN])
    parts = [first] + [s[:, c * BLOCK : (c + 1) * BLOCK] for c in range(1, CHUNKS)]
    top = fold(parts[0], jnp.maximum)
    for c in range(1, CHUNKS):
        y = fold(parts[c], jnp.maximum)
        top = jnp.maximum(top, y if hide is None else y - hide[c])
    top = jnp.max(top, axis=-1, keepdims=True) * RATE
    es = [jnp.exp2(parts[0] * RATE - top)]
    for c in range(1, CHUNKS):
        es.append(jnp.exp2(parts[c] * RATE - (top if hide is None else top + hide[c])))
    total = fold(es[0], jnp.add)
    for e in es[1:]:
        total = total + fold(e, jnp.add)
    inv = 1.0 / jnp.sum(total, axis=-1, keepdims=True)
    gf = read_g().astype(F32)
    gs = (gf * inv).astype(BF)
    eb = [e.astype(BF) for e in es]
    zero = jnp.zeros_like(eb[0])
    eb = jnp.concatenate([jnp.where(old, eb[0], zero)] + eb[1:] + [jnp.where(old, zero, eb[0])], axis=1)
    out = (dot(eb, values, 1, 0) * inv).astype(BF)
    delta = jnp.sum(gf * out.astype(F32), axis=-1, keepdims=True) * inv
    dp = dot(gs, values, 1, 1)
    dparts = [jnp.where(old, dp[:, 0:BLOCK], dp[:, WINDOW:SPAN])]
    dparts += [dp[:, c * BLOCK : (c + 1) * BLOCK] for c in range(1, CHUNKS)]
    ds = [(e * (x - delta)).astype(BF) for e, x in zip(es, dparts)]
    ds = jnp.concatenate([jnp.where(old, ds[0], zero)] + ds[1:] + [jnp.where(old, zero, ds[0])], axis=1)
    dq = (dot(ds, keys, 1, 0) * SCALE).astype(BF)
    return out, dq, (q, ds, gs, eb)


def attend_half(qs, row0, gs, g0, ka, a0, kb, b0, hide_when, acc, put, done, arrive=None):
    row = lax.broadcasted_iota(jnp.int32, (BLOCK, BLOCK), 0)
    col = lax.broadcasted_iota(jnp.int32, (BLOCK, BLOCK), 1)
    old = col > row
    for b in range(CHUNKS):
        r = b * BLOCK
        keys = jnp.concatenate([ka[a0 + r : a0 + WINDOW, 0:D], kb[b0 : b0 + r + BLOCK, 0:D]], axis=0)
        values = jnp.concatenate([ka[a0 + r : a0 + WINDOW, D : 2 * D], kb[b0 : b0 + r + BLOCK, D : 2 * D]], axis=0)
        hide = None
        if hide_when is not None:
            hide = [jnp.where(hide_when, 1e30, 0.0).astype(F32) if b + c < CHUNKS else 0.0 for c in range(CHUNKS)]
        q = qs[row0 + r : row0 + r + BLOCK, :]

        def read_g():
            if r == 0 and arrive is not None:
                arrive.wait()
            return gs[g0 + r : g0 + r + BLOCK, :]

        out, dq, (q, ds, g, eb) = attend(q, read_g, keys, values, old, hide)
        put(r, out, dq)
        seen = 0 if b == 0 else WINDOW
        for i, part in enumerate((dot(q, ds, 0, 0), dot(g, eb, 0, 0))):
            if seen:
                acc[i, :, r : r + seen] += part[:, 0:seen]
            acc[i, :, r + seen : r + SPAN] = part[:, seen:SPAN]
        if done is not None:
            done(r)


def store_rows(ref, row0):
    def put(r, out, dq):
        ref[row0 + r : row0 + r + BLOCK, 0:D] = out
        ref[row0 + r : row0 + r + BLOCK, D : 2 * D] = dq

    return put


def sender(rows, od, row0, acc, sums, sems):
    copies = []

    def send(src, dst):
        copies.append(pltpu.make_async_copy(src, dst, sems.at[len(copies)]))
        copies[-1].start()

    def done(r):
        if r < WINDOW - 2 * BLOCK:
            return
        for r in range(0, r + BLOCK, BLOCK) if r + BLOCK < WINDOW else [r]:
            ship(r)

    def ship(r):
        send(rows.at[pl.ds(r, BLOCK)], od.at[pl.ds(row0 + r, BLOCK), pl.ds(0, 2 * D)])
        if sums is not None:
            cols = pl.ds(r, BLOCK if r + BLOCK < WINDOW else SPAN)
            send(acc.at[:, :, cols], sums.at[:, :, cols])

    return copies, done


def wait_all(copies):
    for copy in copies:
        copy.wait()


LOW, HIGH = slice(0, WINDOW), slice(WINDOW, 2 * WINDOW)
LOW_COLS, HIGH_COLS = pl.ds(0, WINDOW), pl.ds(WINDOW, WINDOW)
GRADS = pl.ds(2 * D, 2 * D)
SCALES = (SCALE, 1.0)


def second_of_first_head(data, od, sums, acc, rows, sems):
    copies, done = sender(rows, od, WINDOW, acc, sums, sems)
    attend_half(data.at[:, 2 * D : 3 * D], WINDOW, data.at[:, 3 * D : 4 * D], WINDOW, data, 0, data, WINDOW, None, acc, store_rows(rows, 0), done)
    wait_all(copies)


def first_of_first_head(lead, data, halo, _, od, sums, acc, rows, sems):
    copies, done = sender(rows, od, 0, acc, sums, sems)
    attend_half(data.at[:, 2 * D : 3 * D], 0, data.at[:, 3 * D : 4 * D], 0, halo, 0, data, 0, lead[0] == 1, acc, store_rows(rows, 0), done)
    wait_all(copies)


def first_of_second_head(lead, data, last_g, halo, before, out, back, own, acc, rows, sums, cotangents, sems):
    load = pltpu.make_async_copy(before.at[:, :, LOW_COLS], sums, sems.at[CHUNKS])
    load.start()
    copies, done = sender(rows, out, 0, acc, None, sems)
    arrive = pltpu.make_async_copy(last_g.at[LOW_COLS], cotangents, sems.at[2 * CHUNKS])
    arrive.start()
    attend_half(data.at[:, 4 * D : 5 * D], 0, cotangents, 0, halo, 0, data, 0, lead[0] == 1, acc, store_rows(rows, 0), done, arrive)
    copies.append(pltpu.make_async_copy(acc.at[:, :, HIGH_COLS], own, sems.at[CHUNKS + 1]))
    copies[-1].start()
    load.wait()
    for i in range(2):
        back[i] = ((acc[i, :, LOW] + sums[i]) * SCALES[i]).astype(BF)
    wait_all(copies)


def second_of_second_head(data, last_g, _, sums_s0, sums_f0, sums_f1, out, last, acc, rows, sums, more, most, grads, cotangents, sems):
    loads = [
        pltpu.make_async_copy(sums_s0, sums, sems.at[CHUNKS]),
        pltpu.make_async_copy(sums_f0.at[:, :, HIGH_COLS], more, sems.at[CHUNKS + 1]),
        pltpu.make_async_copy(sums_f1, most, sems.at[CHUNKS + 2]),
    ]
    for load in loads:
        load.start()
    copies, done = sender(rows, out, WINDOW, acc, None, sems)
    arrive = pltpu.make_async_copy(last_g.at[HIGH_COLS], cotangents, sems.at[2 * CHUNKS])
    arrive.start()
    attend_half(data.at[:, 4 * D : 5 * D], WINDOW, cotangents, 0, data, 0, data, WINDOW, None, acc, store_rows(rows, 0), done, arrive)
    wait_all(loads)
    for i in range(2):
        total = (acc[i, :, LOW] + sums[i, :, LOW]) + (more[i] + most[i])
        grads[:, i * D : (i + 1) * D] = (total.T * SCALES[i]).astype(BF)
    copies.append(pltpu.make_async_copy(grads, out.at[LOW_COLS, GRADS], sems.at[CHUNKS + 3]))
    copies[-1].start()
    for i in range(2):
        last[i] = (acc[i, :, HIGH] + sums[i, :, HIGH]) * SCALES[i]
    wait_all(copies)


def join_gradients(last, more, _, out, grads, sem):
    for i in range(2):
        grads[:, i * D : (i + 1) * D] = (last[i] + more[i].astype(F32)).T.astype(BF)
    copy = pltpu.make_async_copy(grads, out.at[HIGH_COLS, GRADS], sem.at[0])
    copy.start()
    copy.wait()


def call(kernel, operands, in_specs, outs, out_specs, scratch, aliases=None):
    pairs = WINDOW * SPAN
    operands = [pltpu.with_memory_space_constraint(x, pltpu.HBM) if spec is AWAY else x for x, spec in zip(operands, in_specs)]
    return pl.pallas_call(
        kernel,
        in_specs=in_specs,
        out_specs=out_specs,
        out_shape=[pltpu.HBM(*out) if spec is AWAY else jax.ShapeDtypeStruct(*out) for out, spec in zip(outs, out_specs)],
        scratch_shapes=[pltpu.VMEM(SUMS, F32)] + scratch + [pltpu.SemaphoreType.DMA((2 * CHUNKS + 1,))],
        input_output_aliases=aliases or {},
        compiler_params=pltpu.CompilerParams(vmem_limit_bytes=20 * 1024 * 1024),
        cost_estimate=cost(12 * pairs * D, 8e6, pairs),
    )(*operands)


def body(queries, keys, values, output_cotangent):
    axes = ("row", "head")
    heads = lax.axis_size("row") * lax.axis_size("head")
    rows = queries.shape[0]
    groups = lax.axis_size("group")
    tokens = heads * rows
    lead = (lax.axis_index("group") == 0).astype(jnp.int32).reshape(1)

    def spread(x):
        return lax.all_to_all(x, axes, split_axis=0, concat_axis=0, tiled=True)

    part = (2, D, WINDOW)
    sums = (SUMS, F32)
    hold = pltpu.VMEM((WINDOW, 2 * D), BF)
    cotangents = pltpu.VMEM((WINDOW, D), BF)
    first_cuts = [(0, D, 0, D), (1, D, 0, D), (2, 2 * D, 0, D), (3, 2 * D, 0, D), (2, 2 * D, D, D)]
    packed_a = pack([keys, values, queries, output_cotangent], first_cuts, heads)
    packed_b = pack([output_cotangent], [(0, 2 * D, D, D)], heads)
    data = spread(packed_a).reshape(tokens, 5 * D)
    halo = lax.ppermute(data[tokens - WINDOW :, 0 : 2 * D], "group", [(i, i + 1) for i in range(groups - 1)])
    halo = pltpu.with_memory_space_constraint(halo, pltpu.VMEM)
    last_g = spread(packed_b).reshape(tokens, D)
    od_0, sums_s0 = call(second_of_first_head, [data], [VMEM], [((tokens, 2 * D), BF), sums], [AWAY, AWAY], [hold])
    od_0, sums_f0 = call(
        first_of_first_head,
        [lead, data, halo, od_0],
        [SMEM, VMEM, VMEM, AWAY],
        [((tokens, 2 * D), BF), sums],
        [AWAY, AWAY],
        [hold],
        {3: 0},
    )
    out, back, own = call(
        first_of_second_head,
        [lead, data, last_g, halo, sums_f0],
        [SMEM, VMEM, AWAY, VMEM, AWAY],
        [((tokens, 4 * D), BF), (part, BF), (part, F32)],
        [AWAY, VMEM, AWAY],
        [hold, pltpu.VMEM(part, F32), cotangents],
    )
    more = lax.ppermute(back, "group", [(i + 1, i) for i in range(groups - 1)])
    chunks_a = spread(od_0.reshape(heads, rows, 2 * D))
    out, last = call(
        second_of_second_head,
        [data, last_g, out, sums_s0, sums_f0, own],
        [VMEM, AWAY, AWAY, AWAY, AWAY, AWAY],
        [((tokens, 4 * D), BF), (part, F32)],
        [AWAY, VMEM],
        [hold, pltpu.VMEM(SUMS, F32), pltpu.VMEM(part, F32), pltpu.VMEM(part, F32), hold, cotangents],
        {2: 0},
    )
    out = pl.pallas_call(
        join_gradients,
        in_specs=[VMEM, VMEM, AWAY],
        out_specs=AWAY,
        out_shape=pltpu.HBM(out.shape, BF),
        scratch_shapes=[hold, pltpu.SemaphoreType.DMA((1,))],
        input_output_aliases={2: 0},
        compiler_params=pltpu.CompilerParams(vmem_limit_bytes=20 * 1024 * 1024),
        cost_estimate=cost(0, 4e6),
        name="join_gradients",
    )(last, more, pltpu.with_memory_space_constraint(out, pltpu.HBM))
    chunks_b = spread(out.reshape(heads, rows, 4 * D))
    chunks_a = stage(chunks_a)
    return unpack(
        [chunks_a, chunks_b],
        [[(0, 2 * D, 0, D), (1, 2 * D, 0, D)], [(0, 2 * D, D, D), (1, 2 * D, D, D), (2, D, 0, D), (3, D, 0, D)]],
        [2 * D, 2 * D, D, D],
    )


def solution(mesh):
    row = 4
    seq, head = mesh.devices.shape
    finer = Mesh(mesh.devices.reshape(seq // row, row, head), ("group", "row", "head"))
    spec = P(("group", "row", "head"), None)
    return jax.shard_map(body, mesh=finer, in_specs=(spec,) * 4, out_specs=(spec,) * 4, check_vma=False)
```

profile of v0, /device:TPU:1, one launch (start us, length us, event | category | flops | bytes accessed | tf_op | source)
XLA Modules:
  0.0 139.0 jit_solution(10822996173786953480)
XLA Ops:
  0.6 3.0 %pack.2 = bf16[16,128,640]{2,1,0:T(8,128)(2,1)} custom-call(bf16[128,2048]{1,0:T(8,128)(2,1)} %refs_0_.2, bf16[128,2048]{1,0:T(8,128)(2,1)} %refs_1_.1, bf16[128,4096]{1,0:T(8,128)(2,1)} %refs_2_.1, bf16[128,4096]{1,0:T(8,128)(2,1)} %refs_0_.3), custom_call_target="tpu_custom_call" | custom-call | bytes 5242880 | tf_op jit(solution)/shard_map/pack/pallas_call | solution.py:66
  3.7 43.1 %all_to_all.20 = bf16[16,128,640]{2,1,0:T(8,128)(2,1)S(1)} all-to-all(bf16[16,128,640]{2,1,0:T(8,128)(2,1)} %pack.2), channel_id=1, replica_groups=mesh['group'=8,'row'=4,'head'=4] {'row','head'}, dimensions={0} | all-to-all | bytes 5242880 | tf_op jit(solution)/shard_map/all_to_all | solution.py:325
  46.7 0.8 slice.4
  47.6 3.1 %collective-permute-start = (bf16[1024,256]{1,0:T(8,128)(2,1)}, bf16[1024,256]{1,0:T(8,128)(2,1)S(1)}, u32[]{:S(2)}, u32[]{:S(2)}) collective-permute-start(bf16[1024,256]{1,0:T(8,128)(2,1)} %slice.4), channel_id=1, source_target_pairs={{0,16},{16,32},{32,48},{48,64},{64,80},{80,96},{96,112},{1,17},{17... | collective-permute-start | bytes 1572872 | tf_op jit(solution)/shard_map/ppermute | solution.py:335
  50.7 1.9 %pack.3 = bf16[16,128,128]{2,1,0:T(8,128)(2,1)} custom-call(bf16[128,4096]{1,0:T(8,128)(2,1)} %refs_0_.3), custom_call_target="tpu_custom_call" | custom-call | bytes 1048576 | tf_op jit(solution)/shard_map/pack/pallas_call | solution.py:66
  52.7 5.5 %all-to-all-start.2 = ((bf16[16,128,128]{2,1,0:T(8,128)(2,1)}), bf16[16,128,128]{2,1,0:T(8,128)(2,1)}, u32[]{:S(2)}, u32[]{:S(2)}) async-start(bf16[16,128,128]{2,1,0:T(8,128)(2,1)} %pack.3), calls=%async_computation.2 | async-start | bytes 1048576 | tf_op jit(solution)/shard_map/all_to_all | solution.py:325
  58.2 6.1 %shard_map.75 = (bf16[2048,256]{1,0:T(8,128)(2,1)}, f32[2,128,2048]{2,1,0:T(8,128)}) custom-call(bf16[2048,640]{1,0:T(8,128)(2,1)S(1)} %bitcast.6), custom_call_target="tpu_custom_call" | custom-call | flops 2013265920 | bytes 8000000 | tf_op jit(solution)/shard_map/pallas_call | solution.py:304
  64.3 0.0 collective-permute-done.halo
  64.3 6.1 %shard_map.76 = (bf16[2048,256]{1,0:T(8,128)(2,1)}, f32[2,128,2048]{2,1,0:T(8,128)}) custom-call(s32[1]{0:T(128)} %bitcast.lead, bf16[2048,640]{1,0:T(8,128)(2,1)S(1)} %bitcast.7, bf16[1024,256]{1,0:T(8,128)(2,1)S(1)} %collective-permute-done.halo, bf16[2048,256]{1,0:T(8,128)(2,1)} %get-tuple-element.13._), custom_call_target="tpu_custom_call", output_to_operand_aliasing={{0}: (3, {})} | custom-call | flops 2013265920 | bytes 8000000 | tf_op jit(solution)/shard_map/pallas_call | solution.py:304
  70.3 1.8 %all-to-all-done.2 = bf16[16,128,128]{2,1,0:T(8,128)(2,1)} async-done(((bf16[16,128,128]{2,1,0:T(8,128)(2,1)}), bf16[16,128,128]{2,1,0:T(8,128)(2,1)}, u32[]{:S(2)}, u32[]{:S(2)}) %all-to-all-start.2) | async-done | bytes 524320 | tf_op jit(solution)/shard_map/all_to_all | solution.py:325
  72.1 5.5 %all-to-all-start.1 = ((bf16[16,128,256]{2,1,0:T(8,128)(2,1)}), bf16[16,128,256]{2,1,0:T(8,128)(2,1)}, u32[]{:S(2)}, u32[]{:S(2)}) async-start(bf16[16,128,256]{2,1,0:T(8,128)(2,1)} %bitcast.11), calls=%async_computation.1 | async-start | bytes 2097152 | tf_op jit(solution)/shard_map/all_to_all | solution.py:325
  77.7 6.8 %shard_map.77 = (bf16[2048,512]{1,0:T(8,128)(2,1)}, bf16[2,128,1024]{2,1,0:T(8,128)(2,1)S(1)}, f32[2,128,1024]{2,1,0:T(8,128)}) custom-call(s32[1]{0:T(128)} %bitcast.lead, bf16[2048,640]{1,0:T(8,128)(2,1)S(1)} %bitcast.8, bf16[2048,128]{1,0:T(8,128)(2,1)} %bitcast.3.last_g, bf16[1024,256]{1,0:T(8,128)(2,1)S(1)} %collective-permute-done.halo, ...), custom_call_target="tpu_custom_call" | custom-call | flops 2013265920 | bytes 8000000 | tf_op jit(solution)/shard_map/pallas_call | solution.py:304
  84.4 1.3 collective-permute-start.1
  85.7 7.9 %shard_map.78 = (bf16[2048,512]{1,0:T(8,128)(2,1)}, f32[2,128,1024]{2,1,0:T(8,128)S(1)}) custom-call(bf16[2048,640]{1,0:T(8,128)(2,1)S(1)} %bitcast.9, bf16[2048,128]{1,0:T(8,128)(2,1)} %bitcast.3.last_g, bf16[2048,512]{1,0:T(8,128)(2,1)} %get-tuple-element.16._, f32[2,128,2048]{2,1,0:T(8,128)} %get-tuple-element.17.sums_s0, ...), custom_call_target="tpu_custom_call", output_to_operand_aliasing={{0}: (2, {})} | custom-call | flops 2013265920 | bytes 8000000 | tf_op jit(solution)/shard_map/pallas_call | solution.py:304
  93.6 6.0 %collective-permute-done.1.more = bf16[2,128,1024]{2,1,0:T(8,128)(2,1)S(1)} collective-permute-done((bf16[2,128,1024]{2,1,0:T(8,128)(2,1)S(1)}, bf16[2,128,1024]{2,1,0:T(8,128)(2,1)S(1)}, u32[]{:S(2)}, u32[]{:S(2)}) %collective-permute-start.1) | collective-permute-done | bytes 524320 | tf_op jit(solution)/shard_map/ppermute | solution.py:356
  99.6 1.1 join_gradients.1
  100.7 0.0 all-to-all-done.1.src
  100.7 7.9 %all-to-all-start.3 = ((bf16[16,128,512]{2,1,0:T(8,128)(2,1)}), bf16[16,128,512]{2,1,0:T(8,128)(2,1)S(1)}, u32[]{:S(2)}, u32[]{:S(2)}) async-start(bf16[16,128,512]{2,1,0:T(8,128)(2,1)} %bitcast.10), calls=%async_computation.3 | async-start | bytes 4194304 | tf_op jit(solution)/shard_map/all_to_all | solution.py:325
  108.6 1.2 stage.1.refs_0_
  109.8 27.1 %all-to-all-done.3.refs_1_ = bf16[16,128,512]{2,1,0:T(8,128)(2,1)S(1)} async-done(((bf16[16,128,512]{2,1,0:T(8,128)(2,1)}), bf16[16,128,512]{2,1,0:T(8,128)(2,1)S(1)}, u32[]{:S(2)}, u32[]{:S(2)}) %all-to-all-start.3) | async-done | bytes 2097184 | tf_op jit(solution)/shard_map/all_to_all | solution.py:325
  136.9 1.9 %unpack.1 = (bf16[128,4096]{1,0:T(8,128)(2,1)}, bf16[128,4096]{1,0:T(8,128)(2,1)}, bf16[128,2048]{1,0:T(8,128)(2,1)}, bf16[128,2048]{1,0:T(8,128)(2,1)}) custom-call(bf16[16,128,256]{2,1,0:T(8,128)(2,1)S(1)} %stage.1.refs_0_, bf16[16,128,512]{2,1,0:T(8,128)(2,1)S(1)} %all-to-all-done.3.refs_1_), custom_call_target="tpu_custom_call" | custom-call | bytes 6291456 | tf_op jit(solution)/shard_map/unpack/pallas_call | solution.py:99
Async XLA Ops:
  47.6 16.7 %collective-permute-start = (bf16[1024,256]{1,0:T(8,128)(2,1)}, bf16[1024,256]{1,0:T(8,128)(2,1)S(1)}, u32[]{:S(2)}, u32[]{:S(2)}) collective-permute-start(bf16[1024,256]{1,0:T(8,128)(2,1)} %slice.4), channel_id=1, source_target_pairs={{0,16},{16,32},{32,48},{48,64},{64,80},{80,96},{96,112},{1,17},{17... | collective-permute-start | bytes 1572872 | tf_op jit(solution)/shard_map/ppermute | solution.py:335
  52.7 19.4 %all-to-all-start.2 = ((bf16[16,128,128]{2,1,0:T(8,128)(2,1)}), bf16[16,128,128]{2,1,0:T(8,128)(2,1)}, u32[]{:S(2)}, u32[]{:S(2)}) async-start(bf16[16,128,128]{2,1,0:T(8,128)(2,1)} %pack.3), calls=%async_computation.2 | async-start | bytes 1048576 | tf_op jit(solution)/shard_map/all_to_all | solution.py:325
  72.1 28.6 %all-to-all-start.1 = ((bf16[16,128,256]{2,1,0:T(8,128)(2,1)}), bf16[16,128,256]{2,1,0:T(8,128)(2,1)}, u32[]{:S(2)}, u32[]{:S(2)}) async-start(bf16[16,128,256]{2,1,0:T(8,128)(2,1)} %bitcast.11), calls=%async_computation.1 | async-start | bytes 2097152 | tf_op jit(solution)/shard_map/all_to_all | solution.py:325
  84.4 15.2 %collective-permute-start.1 = (bf16[2,128,1024]{2,1,0:T(8,128)(2,1)S(1)}, bf16[2,128,1024]{2,1,0:T(8,128)(2,1)S(1)}, u32[]{:S(2)}, u32[]{:S(2)}) collective-permute-start(bf16[2,128,1024]{2,1,0:T(8,128)(2,1)S(1)} %get-tuple-element.20), channel_id=1, source_target_pairs={{16,0},{32,16},{48,32},{64,48},{80,64},{96,80},{112,96},{17,1},{33... | collective-permute-start | bytes 1572872 | tf_op jit(solution)/shard_map/ppermute | solution.py:356
  100.7 36.2 %all-to-all-start.3 = ((bf16[16,128,512]{2,1,0:T(8,128)(2,1)}), bf16[16,128,512]{2,1,0:T(8,128)(2,1)S(1)}, u32[]{:S(2)}, u32[]{:S(2)}) async-start(bf16[16,128,512]{2,1,0:T(8,128)(2,1)} %bitcast.10), calls=%async_computation.3 | async-start | bytes 4194304 | tf_op jit(solution)/shard_map/all_to_all | solution.py:325
where the time goes:
time: 140 us; the launch traced here: 139 us
  blocking collectives  43.1 us (31%)
  Pallas kernels  36 us (26%)
  waiting for transfers between devices  34.9 us (25%)
  starting transfers between devices  23.4 us (17%)
    all_to_all x1, blocking collectives, spread(): return lax.all_to_all(x, axes, split_axis=0, concat_axis=0, tiled=True)  43.1 us
    all_to_all x3, waiting for transfers between devices, spread(): return lax.all_to_all(x, axes, split_axis=0, concat_axis=0, tiled=True)  28.9 us
    pallas_call x4, Pallas kernels, call(): pl.pallas_call(kernel, in_specs=in_specs, out_specs=out_specs, out_shape=...  26.8 us
    all_to_all x3, starting transfers between devices, spread(): return lax.all_to_all(x, axes, split_axis=0, concat_axis=0, tiled=True)  18.9 us
    ppermute x1, waiting for transfers between devices, body(): more = lax.ppermute(back, 'group', [(i + 1, i) for i in range(groups - 1)])  6 us
    pallas_call x2, Pallas kernels, pack(): pl.pallas_call(kernel, in_specs=[AWAY] * n, out_specs=AWAY, out_shape=plt...  4.96 us
    ppermute x1, starting transfers between devices, body(): lax.ppermute(data[tokens - WINDOW:, 0:2 * D], 'group', [(i, i + 1) for i...  3.14 us
  transfers between devices with their start and end apart: 5, of which 3 were waited for; matrix products, arithmetic and copies ran while one was open for 0% of the time, Pallas kernels for 22%

commit v1 on v0

--- a/solution.py
+++ b/solution.py
@@ -27,7 +27,7 @@
 SUMS = (2, D, 2 * WINDOW)
 
 
-PIECES = 4
+PIECES = 2
 
 
 def strips(cuts, heads):
@@ -138,7 +138,7 @@
     return y
 
 
-def attend(q, read_g, keys, values, old, hide):
+def attend(q, g, keys, values, old, hide):
     s = dot(q, keys, 1, 1)
     first = jnp.where(old, s[:, 0:BLOCK] if hide is None else s[:, 0:BLOCK] - hide[0], s[:, WINDOW:SPAN])
     parts = [first] + [s[:, c * BLOCK : (c + 1) * BLOCK] for c in range(1, CHUNKS)]
@@ -154,7 +154,7 @@
     for e in es[1:]:
         total = total + fold(e, jnp.add)
     inv = 1.0 / jnp.sum(total, axis=-1, keepdims=True)
-    gf = read_g().astype(F32)
+    gf = g.astype(F32)
     gs = (gf * inv).astype(BF)
     eb = [e.astype(BF) for e in es]
     zero = jnp.zeros_like(eb[0])
@@ -170,7 +170,7 @@
     return out, dq, (q, ds, gs, eb)
 
 
-def attend_half(qs, row0, gs, g0, ka, a0, kb, b0, hide_when, acc, put, done, arrive=None):
+def attend_half(qg, row0, ka, a0, kb, b0, hide_when, acc, put, done=None):
     row = lax.broadcasted_iota(jnp.int32, (BLOCK, BLOCK), 0)
     col = lax.broadcasted_iota(jnp.int32, (BLOCK, BLOCK), 1)
     old = col > row
@@ -181,17 +181,12 @@
         hide = None
         if hide_when is not None:
             hide = [jnp.where(hide_when, 1e30, 0.0).astype(F32) if b + c < CHUNKS else 0.0 for c in range(CHUNKS)]
-        q = qs[row0 + r : row0 + r + BLOCK, :]
-
-        def read_g():
-            if r == 0 and arrive is not None:
-                arrive.wait()
-            return gs[g0 + r : g0 + r + BLOCK, :]
-
-        out, dq, (q, ds, g, eb) = attend(q, read_g, keys, values, old, hide)
+        q = qg[row0 + r : row0 + r + BLOCK, 0:D]
+        g = qg[row0 + r : row0 + r + BLOCK, D : 2 * D]
+        out, dq, (q, ds, gs, eb) = attend(q, g, keys, values, old, hide)
         put(r, out, dq)
         seen = 0 if b == 0 else WINDOW
-        for i, part in enumerate((dot(q, ds, 0, 0), dot(g, eb, 0, 0))):
+        for i, part in enumerate((dot(q, ds, 0, 0), dot(gs, eb, 0, 0))):
             if seen:
                 acc[i, :, r : r + seen] += part[:, 0:seen]
             acc[i, :, r + seen : r + SPAN] = part[:, seen:SPAN]
@@ -215,12 +210,6 @@
         copies[-1].start()
 
     def done(r):
-        if r < WINDOW - 2 * BLOCK:
-            return
-        for r in range(0, r + BLOCK, BLOCK) if r + BLOCK < WINDOW else [r]:
-            ship(r)
-
-    def ship(r):
         send(rows.at[pl.ds(r, BLOCK)], od.at[pl.ds(row0 + r, BLOCK), pl.ds(0, 2 * D)])
         if sums is not None:
             cols = pl.ds(r, BLOCK if r + BLOCK < WINDOW else SPAN)
@@ -240,25 +229,23 @@
 SCALES = (SCALE, 1.0)
 
 
-def second_of_first_head(data, od, sums, acc, rows, sems):
+def second_of_first_head(kvqg, od, sums, acc, rows, sems):
     copies, done = sender(rows, od, WINDOW, acc, sums, sems)
-    attend_half(data.at[:, 2 * D : 3 * D], WINDOW, data.at[:, 3 * D : 4 * D], WINDOW, data, 0, data, WINDOW, None, acc, store_rows(rows, 0), done)
+    attend_half(kvqg.at[:, 2 * D : 4 * D], WINDOW, kvqg, 0, kvqg, WINDOW, None, acc, store_rows(rows, 0), done)
     wait_all(copies)
 
 
-def first_of_first_head(lead, data, halo, _, od, sums, acc, rows, sems):
+def first_of_first_head(lead, kvqg, halo, _, od, sums, acc, rows, sems):
     copies, done = sender(rows, od, 0, acc, sums, sems)
-    attend_half(data.at[:, 2 * D : 3 * D], 0, data.at[:, 3 * D : 4 * D], 0, halo, 0, data, 0, lead[0] == 1, acc, store_rows(rows, 0), done)
+    attend_half(kvqg.at[:, 2 * D : 4 * D], 0, halo, 0, kvqg, 0, lead[0] == 1, acc, store_rows(rows, 0), done)
     wait_all(copies)
 
 
-def first_of_second_head(lead, data, last_g, halo, before, out, back, own, acc, rows, sums, cotangents, sems):
+def first_of_second_head(lead, kvqg, qg, halo, before, out, back, own, acc, rows, sums, sems):
     load = pltpu.make_async_copy(before.at[:, :, LOW_COLS], sums, sems.at[CHUNKS])
     load.start()
     copies, done = sender(rows, out, 0, acc, None, sems)
-    arrive = pltpu.make_async_copy(last_g.at[LOW_COLS], cotangents, sems.at[2 * CHUNKS])
-    arrive.start()
-    attend_half(data.at[:, 4 * D : 5 * D], 0, cotangents, 0, halo, 0, data, 0, lead[0] == 1, acc, store_rows(rows, 0), done, arrive)
+    attend_half(qg, 0, halo, 0, kvqg, 0, lead[0] == 1, acc, store_rows(rows, 0), done)
     copies.append(pltpu.make_async_copy(acc.at[:, :, HIGH_COLS], own, sems.at[CHUNKS + 1]))
     copies[-1].start()
     load.wait()
@@ -267,7 +254,7 @@
     wait_all(copies)
 
 
-def second_of_second_head(data, last_g, _, sums_s0, sums_f0, sums_f1, out, last, acc, rows, sums, more, most, grads, cotangents, sems):
+def second_of_second_head(kvqg, qg, _, sums_s0, sums_f0, sums_f1, out, last, acc, rows, sums, more, most, grads, sems):
     loads = [
         pltpu.make_async_copy(sums_s0, sums, sems.at[CHUNKS]),
         pltpu.make_async_copy(sums_f0.at[:, :, HIGH_COLS], more, sems.at[CHUNKS + 1]),
@@ -276,9 +263,7 @@
     for load in loads:
         load.start()
     copies, done = sender(rows, out, WINDOW, acc, None, sems)
-    arrive = pltpu.make_async_copy(last_g.at[HIGH_COLS], cotangents, sems.at[2 * CHUNKS])
-    arrive.start()
-    attend_half(data.at[:, 4 * D : 5 * D], WINDOW, cotangents, 0, data, 0, data, WINDOW, None, acc, store_rows(rows, 0), done, arrive)
+    attend_half(qg, WINDOW, kvqg, 0, kvqg, WINDOW, None, acc, store_rows(rows, 0), done)
     wait_all(loads)
     for i in range(2):
         total = (acc[i, :, LOW] + sums[i, :, LOW]) + (more[i] + most[i])
@@ -327,18 +312,16 @@
     part = (2, D, WINDOW)
     sums = (SUMS, F32)
     hold = pltpu.VMEM((WINDOW, 2 * D), BF)
-    cotangents = pltpu.VMEM((WINDOW, D), BF)
-    first_cuts = [(0, D, 0, D), (1, D, 0, D), (2, 2 * D, 0, D), (3, 2 * D, 0, D), (2, 2 * D, D, D)]
+    first_cuts = [(0, D, 0, D), (1, D, 0, D), (2, 2 * D, 0, D), (3, 2 * D, 0, D)]
     packed_a = pack([keys, values, queries, output_cotangent], first_cuts, heads)
-    packed_b = pack([output_cotangent], [(0, 2 * D, D, D)], heads)
-    data = spread(packed_a).reshape(tokens, 5 * D)
-    halo = lax.ppermute(data[tokens - WINDOW :, 0 : 2 * D], "group", [(i, i + 1) for i in range(groups - 1)])
-    halo = pltpu.with_memory_space_constraint(halo, pltpu.VMEM)
-    last_g = spread(packed_b).reshape(tokens, D)
-    od_0, sums_s0 = call(second_of_first_head, [data], [VMEM], [((tokens, 2 * D), BF), sums], [AWAY, AWAY], [hold])
+    packed_b = pack([queries, output_cotangent], [(0, 2 * D, D, D), (1, 2 * D, D, D)], heads)
+    kvqg = spread(packed_a).reshape(tokens, 4 * D)
+    halo = lax.ppermute(kvqg[tokens - WINDOW :, 0 : 2 * D], "group", [(i, i + 1) for i in range(groups - 1)])
+    qg = spread(packed_b).reshape(tokens, 2 * D)
+    od_0, sums_s0 = call(second_of_first_head, [kvqg], [VMEM], [((tokens, 2 * D), BF), sums], [AWAY, AWAY], [hold])
     od_0, sums_f0 = call(
         first_of_first_head,
-        [lead, data, halo, od_0],
+        [lead, kvqg, halo, od_0],
         [SMEM, VMEM, VMEM, AWAY],
         [((tokens, 2 * D), BF), sums],
         [AWAY, AWAY],
@@ -347,21 +330,21 @@
     )
     out, back, own = call(
         first_of_second_head,
-        [lead, data, last_g, halo, sums_f0],
-        [SMEM, VMEM, AWAY, VMEM, AWAY],
+        [lead, kvqg, qg, halo, sums_f0],
+        [SMEM, VMEM, VMEM, VMEM, AWAY],
         [((tokens, 4 * D), BF), (part, BF), (part, F32)],
         [AWAY, VMEM, AWAY],
-        [hold, pltpu.VMEM(part, F32), cotangents],
+        [hold, pltpu.VMEM(part, F32)],
     )
     more = lax.ppermute(back, "group", [(i + 1, i) for i in range(groups - 1)])
     chunks_a = spread(od_0.reshape(heads, rows, 2 * D))
     out, last = call(
         second_of_second_head,
-        [data, last_g, out, sums_s0, sums_f0, own],
-        [VMEM, AWAY, AWAY, AWAY, AWAY, AWAY],
+        [kvqg, qg, out, sums_s0, sums_f0, own],
+        [VMEM, VMEM, AWAY, AWAY, AWAY, AWAY],
         [((tokens, 4 * D), BF), (part, F32)],
         [AWAY, VMEM],
-        [hold, pltpu.VMEM(SUMS, F32), pltpu.VMEM(part, F32), pltpu.VMEM(part, F32), hold, cotangents],
+        [hold, pltpu.VMEM(SUMS, F32), pltpu.VMEM(part, F32), pltpu.VMEM(part, F32), hold],
         {2: 0},
     )
     out = pl.pallas_call(

time: 140 us -> 142 us (1.014)
  blocking collectives: 43.1 us -> 0 us
  waiting for transfers between devices: 34.9 us -> 70.9 us
  starting transfers between devices: 23.4 us -> 32.4 us
    all_to_all x1 -> x0, blocking collectives: 43.1 us -> none  [spread(): return lax.all_to_all(x, axes, split_axis=0, concat_axis=0, tiled=True)]
    all_to_all x3 -> x4, waiting for transfers between devices: 28.9 us -> 59 us  [spread(): return lax.all_to_all(x, axes, split_axis=0, concat_axis=0, tiled=True)]
    all_to_all x3 -> x4, starting transfers between devices: 18.9 us -> 27.2 us  [spread(): return lax.all_to_all(x, axes, split_axis=0, concat_axis=0, tiled=True)]
    ppermute x1, waiting for transfers between devices: 0.01 us -> 4.52 us  [body(): lax.ppermute(kvqg[tokens - WINDOW:, 0:2 * D], 'group', [(i, i + 1) for i...]
    ppermute x1, waiting for transfers between devices: 6 us -> 7.43 us  [body(): more = lax.ppermute(back, 'group', [(i + 1, i) for i in range(groups - 1)])]
  transfers between devices with their start and end apart: 5 -> 6, of which waited for: 3 -> 5; matrix products, arithmetic and copies ran while one was open for 0% -> 1% of each run, Pallas kernels for 22% -> 22%
where the time goes in v1:
time: 142 us; the launch traced here: 141 us
  waiting for transfers between devices  70.9 us (50%)
  Pallas kernels  36.1 us (25%)
  starting transfers between devices  32.4 us (23%)
    all_to_all x4, waiting for transfers between devices, spread(): return lax.all_to_all(x, axes, split_axis=0, concat_axis=0, tiled=True)  59 us
    all_to_all x4, starting transfers between devices, spread(): return lax.all_to_all(x, axes, split_axis=0, concat_axis=0, tiled=True)  27.2 us
    pallas_call x4, Pallas kernels, call(): pl.pallas_call(kernel, in_specs=in_specs, out_specs=out_specs, out_shape=...  26.3 us
    ppermute x1, waiting for transfers between devices, body(): more = lax.ppermute(back, 'group', [(i + 1, i) for i in range(groups - 1)])  7.43 us
    pallas_call x2, Pallas kernels, pack(): pl.pallas_call(kernel, in_specs=[AWAY] * n, out_specs=AWAY, out_shape=plt...  5.56 us
    ppermute x1, waiting for transfers between devices, body(): lax.ppermute(kvqg[tokens - WINDOW:, 0:2 * D], 'group', [(i, i + 1) for i...  4.52 us
    ppermute x1, starting transfers between devices, body(): lax.ppermute(kvqg[tokens - WINDOW:, 0:2 * D], 'group', [(i, i + 1) for i...  3.9 us
  transfers between devices with their start and end apart: 6, of which 5 were waited for; matrix products, arithmetic and copies ran while one was open for 1% of the time, Pallas kernels for 22%

profile of v1, /device:TPU:1, one launch (start us, length us, event | category | flops | bytes accessed | tf_op | source)
XLA Modules:
  0.0 141.2 jit_solution(9575423810904849320)
XLA Ops:
  0.6 3.1 %pack.2 = bf16[16,128,512]{2,1,0:T(8,128)(2,1)} custom-call(bf16[128,2048]{1,0:T(8,128)(2,1)} %refs_0_.2, bf16[128,2048]{1,0:T(8,128)(2,1)} %refs_1_.2, bf16[128,4096]{1,0:T(8,128)(2,1)} %refs_0_.3, bf16[128,4096]{1,0:T(8,128)(2,1)} %refs_1_.3), custom_call_target="tpu_custom_call" | custom-call | bytes 4194304 | tf_op jit(solution)/shard_map/pack/pallas_call | solution.py:66
  3.7 9.5 %all-to-all-start = ((bf16[16,128,512]{2,1,0:T(8,128)(2,1)}), bf16[16,128,512]{2,1,0:T(8,128)(2,1)S(1)}, u32[]{:S(2)}, u32[]{:S(2)}) async-start(bf16[16,128,512]{2,1,0:T(8,128)(2,1)} %pack.2), calls=%async_computation | async-start | bytes 4194304 | tf_op jit(solution)/shard_map/all_to_all | solution.py:310
  13.2 2.5 %pack.3 = bf16[16,128,256]{2,1,0:T(8,128)(2,1)} custom-call(bf16[128,4096]{1,0:T(8,128)(2,1)} %refs_0_.3, bf16[128,4096]{1,0:T(8,128)(2,1)} %refs_1_.3), custom_call_target="tpu_custom_call" | custom-call | bytes 2097152 | tf_op jit(solution)/shard_map/pack/pallas_call | solution.py:66
  15.7 25.9 %all-to-all-done = bf16[16,128,512]{2,1,0:T(8,128)(2,1)S(1)} async-done(((bf16[16,128,512]{2,1,0:T(8,128)(2,1)}), bf16[16,128,512]{2,1,0:T(8,128)(2,1)S(1)}, u32[]{:S(2)}, u32[]{:S(2)}) %all-to-all-start) | async-done | bytes 2097184 | tf_op jit(solution)/shard_map/all_to_all | solution.py:310
  41.6 4.5 %all-to-all-start.2 = ((bf16[16,128,256]{2,1,0:T(8,128)(2,1)}), bf16[16,128,256]{2,1,0:T(8,128)(2,1)S(1)}, u32[]{:S(2)}, u32[]{:S(2)}) async-start(bf16[16,128,256]{2,1,0:T(8,128)(2,1)} %pack.3), calls=%async_computation.2 | async-start | bytes 2097152 | tf_op jit(solution)/shard_map/all_to_all | solution.py:310
  46.0 0.8 slice.4
  46.9 3.9 %collective-permute-start = (bf16[1024,256]{1,0:T(8,128)(2,1)}, bf16[1024,256]{1,0:T(8,128)(2,1)}, u32[]{:S(2)}, u32[]{:S(2)}) collective-permute-start(bf16[1024,256]{1,0:T(8,128)(2,1)} %slice.4), channel_id=1, source_target_pairs={{0,16},{16,32},{32,48},{48,64},{64,80},{80,96},{96,112},{1,17},{17... | collective-permute-start | bytes 1572872 | tf_op jit(solution)/shard_map/ppermute | solution.py:319
  50.8 6.0 %shard_map.75 = (bf16[2048,256]{1,0:T(8,128)(2,1)}, f32[2,128,2048]{2,1,0:T(8,128)}) custom-call(bf16[2048,512]{1,0:T(8,128)(2,1)S(1)} %bitcast.6), custom_call_target="tpu_custom_call" | custom-call | flops 2013265920 | bytes 8000000 | tf_op jit(solution)/shard_map/pallas_call | solution.py:289
  56.8 4.5 %collective-permute-done.halo = bf16[1024,256]{1,0:T(8,128)(2,1)} collective-permute-done((bf16[1024,256]{1,0:T(8,128)(2,1)}, bf16[1024,256]{1,0:T(8,128)(2,1)}, u32[]{:S(2)}, u32[]{:S(2)}) %collective-permute-start) | collective-permute-done | bytes 524320 | tf_op jit(solution)/shard_map/ppermute | solution.py:319
  61.3 7.1 %shard_map.76 = (bf16[2048,256]{1,0:T(8,128)(2,1)}, f32[2,128,2048]{2,1,0:T(8,128)}) custom-call(s32[1]{0:T(128)} %bitcast.lead, bf16[2048,512]{1,0:T(8,128)(2,1)S(1)} %bitcast.7, bf16[1024,256]{1,0:T(8,128)(2,1)} %collective-permute-done.halo, bf16[2048,256]{1,0:T(8,128)(2,1)} %get-tuple-element.13._), custom_call_target="tpu_custom_call", output_to_operand_aliasing={{0}: (3, {})} | custom-call | flops 2013265920 | bytes 8000000 | tf_op jit(solution)/shard_map/pallas_call | solution.py:289
  68.4 6.0 %all-to-all-done.2 = bf16[16,128,256]{2,1,0:T(8,128)(2,1)S(1)} async-done(((bf16[16,128,256]{2,1,0:T(8,128)(2,1)}), bf16[16,128,256]{2,1,0:T(8,128)(2,1)S(1)}, u32[]{:S(2)}, u32[]{:S(2)}) %all-to-all-start.2) | async-done | bytes 1048608 | tf_op jit(solution)/shard_map/all_to_all | solution.py:310
  74.4 5.0 %all-to-all-start.1 = ((bf16[16,128,256]{2,1,0:T(8,128)(2,1)}), bf16[16,128,256]{2,1,0:T(8,128)(2,1)}, u32[]{:S(2)}, u32[]{:S(2)}) async-start(bf16[16,128,256]{2,1,0:T(8,128)(2,1)} %bitcast.13), calls=%async_computation.1 | async-start | bytes 2097152 | tf_op jit(solution)/shard_map/all_to_all | solution.py:310
  79.5 7.0 %shard_map.77 = (bf16[2048,512]{1,0:T(8,128)(2,1)}, bf16[2,128,1024]{2,1,0:T(8,128)(2,1)S(1)}, f32[2,128,1024]{2,1,0:T(8,128)}) custom-call(s32[1]{0:T(128)} %bitcast.lead, bf16[2048,512]{1,0:T(8,128)(2,1)S(1)} %bitcast.8, bf16[2048,256]{1,0:T(8,128)(2,1)S(1)} %bitcast.10, bf16[1024,256]{1,0:T(8,128)(2,1)} %collective-permute-done.halo, ...), custom_call_target="tpu_custom_call" | custom-call | flops 2013265920 | bytes 8000000 | tf_op jit(solution)/shard_map/pallas_call | solution.py:289
  86.4 1.3 collective-permute-start.1
  87.7 6.2 %shard_map.78 = (bf16[2048,512]{1,0:T(8,128)(2,1)}, f32[2,128,1024]{2,1,0:T(8,128)S(1)}) custom-call(bf16[2048,512]{1,0:T(8,128)(2,1)S(1)} %bitcast.9, bf16[2048,256]{1,0:T(8,128)(2,1)S(1)} %bitcast.11, bf16[2048,512]{1,0:T(8,128)(2,1)} %get-tuple-element.16._, f32[2,128,2048]{2,1,0:T(8,128)} %get-tuple-element.17.sums_s0, ...), custom_call_target="tpu_custom_call", output_to_operand_aliasing={{0}: (2, {})} | custom-call | flops 2013265920 | bytes 8000000 | tf_op jit(solution)/shard_map/pallas_call | solution.py:289
  93.9 7.4 %collective-permute-done.1.more = bf16[2,128,1024]{2,1,0:T(8,128)(2,1)S(1)} collective-permute-done((bf16[2,128,1024]{2,1,0:T(8,128)(2,1)S(1)}, bf16[2,128,1024]{2,1,0:T(8,128)(2,1)S(1)}, u32[]{:S(2)}, u32[]{:S(2)}) %collective-permute-start.1) | collective-permute-done | bytes 524320 | tf_op jit(solution)/shard_map/ppermute | solution.py:339
  101.3 1.1 join_gradients.1
  102.4 0.0 all-to-all-done.1.src
  102.4 8.2 %all-to-all-start.3 = ((bf16[16,128,512]{2,1,0:T(8,128)(2,1)}), bf16[16,128,512]{2,1,0:T(8,128)(2,1)S(1)}, u32[]{:S(2)}, u32[]{:S(2)}) async-start(bf16[16,128,512]{2,1,0:T(8,128)(2,1)} %bitcast.12), calls=%async_computation.3 | async-start | bytes 4194304 | tf_op jit(solution)/shard_map/all_to_all | solution.py:310
  110.7 1.2 stage.1.refs_0_
  111.9 27.1 %all-to-all-done.3.refs_1_ = bf16[16,128,512]{2,1,0:T(8,128)(2,1)S(1)} async-done(((bf16[16,128,512]{2,1,0:T(8,128)(2,1)}), bf16[16,128,512]{2,1,0:T(8,128)(2,1)S(1)}, u32[]{:S(2)}, u32[]{:S(2)}) %all-to-all-start.3) | async-done | bytes 2097184 | tf_op jit(solution)/shard_map/all_to_all | solution.py:310
  139.0 2.0 %unpack.1 = (bf16[128,4096]{1,0:T(8,128)(2,1)}, bf16[128,4096]{1,0:T(8,128)(2,1)}, bf16[128,2048]{1,0:T(8,128)(2,1)}, bf16[128,2048]{1,0:T(8,128)(2,1)}) custom-call(bf16[16,128,256]{2,1,0:T(8,128)(2,1)S(1)} %stage.1.refs_0_, bf16[16,128,512]{2,1,0:T(8,128)(2,1)S(1)} %all-to-all-done.3.refs_1_), custom_call_target="tpu_custom_call" | custom-call | bytes 6291456 | tf_op jit(solution)/shard_map/unpack/pallas_call | solution.py:99
Async XLA Ops:
  3.7 37.8 %all-to-all-start = ((bf16[16,128,512]{2,1,0:T(8,128)(2,1)}), bf16[16,128,512]{2,1,0:T(8,128)(2,1)S(1)}, u32[]{:S(2)}, u32[]{:S(2)}) async-start(bf16[16,128,512]{2,1,0:T(8,128)(2,1)} %pack.2), calls=%async_computation | async-start | bytes 4194304 | tf_op jit(solution)/shard_map/all_to_all | solution.py:310
  41.6 32.9 %all-to-all-start.2 = ((bf16[16,128,256]{2,1,0:T(8,128)(2,1)}), bf16[16,128,256]{2,1,0:T(8,128)(2,1)S(1)}, u32[]{:S(2)}, u32[]{:S(2)}) async-start(bf16[16,128,256]{2,1,0:T(8,128)(2,1)} %pack.3), calls=%async_computation.2 | async-start | bytes 2097152 | tf_op jit(solution)/shard_map/all_to_all | solution.py:310
  46.9 14.5 %collective-permute-start = (bf16[1024,256]{1,0:T(8,128)(2,1)}, bf16[1024,256]{1,0:T(8,128)(2,1)}, u32[]{:S(2)}, u32[]{:S(2)}) collective-permute-start(bf16[1024,256]{1,0:T(8,128)(2,1)} %slice.4), channel_id=1, source_target_pairs={{0,16},{16,32},{32,48},{48,64},{64,80},{80,96},{96,112},{1,17},{17... | collective-permute-start | bytes 1572872 | tf_op jit(solution)/shard_map/ppermute | solution.py:319
  74.4 28.0 %all-to-all-start.1 = ((bf16[16,128,256]{2,1,0:T(8,128)(2,1)}), bf16[16,128,256]{2,1,0:T(8,128)(2,1)}, u32[]{:S(2)}, u32[]{:S(2)}) async-start(bf16[16,128,256]{2,1,0:T(8,128)(2,1)} %bitcast.13), calls=%async_computation.1 | async-start | bytes 2097152 | tf_op jit(solution)/shard_map/all_to_all | solution.py:310
  86.4 14.9 %collective-permute-start.1 = (bf16[2,128,1024]{2,1,0:T(8,128)(2,1)S(1)}, bf16[2,128,1024]{2,1,0:T(8,128)(2,1)S(1)}, u32[]{:S(2)}, u32[]{:S(2)}) collective-permute-start(bf16[2,128,1024]{2,1,0:T(8,128)(2,1)S(1)} %get-tuple-element.20), channel_id=1, source_target_pairs={{16,0},{32,16},{48,32},{64,48},{80,64},{96,80},{112,96},{17,1},{33... | collective-permute-start | bytes 1572872 | tf_op jit(solution)/shard_map/ppermute | solution.py:339
  102.4 36.6 %all-to-all-start.3 = ((bf16[16,128,512]{2,1,0:T(8,128)(2,1)}), bf16[16,128,512]{2,1,0:T(8,128)(2,1)S(1)}, u32[]{:S(2)}, u32[]{:S(2)}) async-start(bf16[16,128,512]{2,1,0:T(8,128)(2,1)} %bitcast.12), calls=%async_computation.3 | async-start | bytes 4194304 | tf_op jit(solution)/shard_map/all_to_all | solution.py:310
